TPU v7x, 512 devices: a whole 4x4x16 slice. The times are simulated.
512 devices in a mesh: table: 64 (over y, z), dp: 8 (over x, core).
Axes of the slice: x: 4, y: 4, z: 16, core: 2. Of those that a mesh axis runs over, the one named last changes fastest.
Arguments:
- table: bfloat16 [24576, 512], P('table'), may hold values from -6 to 6
- owner: int32 [512, 256, 1], P(('table', 'dp')), may hold values from 0 to 63; in each aligned block of 256 rows (0 to 255, 256 to 511, ..., all dimensions but the last counted through in order) at most 8 rows name the same one
- row_in_shard: int32 [512, 256], P(('table', 'dp')), may hold values from 0 to 383
- segment: int32 [512, 256], P(('table', 'dp')), may hold values from 0 to 3, never falling along the last dimension, each value on 1 to 128 neighbouring positions
- w_in: bfloat16 [512, 2048], replicated, may hold values from -0.25 to 0.25
- w_out: bfloat16 [512, 512], replicated, may hold values from -0.25 to 0.25
- cotangent: bfloat16 [512, 256, 512], P(('table', 'dp')), may hold values from -6 to 6
Outputs:
- layer_out: bfloat16 [512, 256, 512], P(('table', 'dp'))
- grad_table: float32 [24576, 512], P('table')
- grad_w_in: float32 [512, 2048], P(None, 'dp')
- grad_w_out: float32 [512, 512], P('dp')
Inputs may be any that keep to these rules, and one draw needn't show every extreme that they name: `owner`: among one device's 256 positions no shard is named more than 8 times, a bound that some block reaches. `segment`: never falls along a buffer; each history has 1 to 128 positions and one has exactly 128.
All inputs are finite; a program needn't handle non-finite values.
Results may differ from a plain program's by a relative error of at most 0.019.
Values may be sent and summed in bfloat16 or wider, within the bound.
No kernel may reach another device: no remote copies, remote signals or barrier semaphores. Data moves between devices by JAX's collectives and lax.ppermute only.
A program may use at most 64 MiB of HBM per device.

v0:
```python
import jax
import jax.numpy as jnp
from jax import lax
from jax.sharding import PartitionSpec as P

HEADS = 8


EPS = 1e-05


def normalize(values):
    average = jnp.mean(values, axis=-1, keepdims=True)
    centred = values - average
    spread = jnp.mean(centred * centred, axis=-1, keepdims=True)
    return centred * lax.rsqrt(spread + EPS)


def hstu_layer(embedded, w_in, w_out, segment):
    row_count, width = embedded.shape
    head_size = width // HEADS
    normed = normalize(embedded.astype(jnp.float32)).astype(jnp.bfloat16)
    mixed_all = jax.nn.silu(jnp.dot(normed, w_in, preferred_element_type=jnp.float32)).astype(
        jnp.bfloat16
    )
    gate_part = mixed_all[:, :width]
    value_part = mixed_all[:, width : 2 * width].reshape(row_count, HEADS, head_size)
    query_part = mixed_all[:, 2 * width : 3 * width].reshape(row_count, HEADS, head_size)
    key_part = mixed_all[:, 3 * width :].reshape(row_count, HEADS, head_size)
    position = jnp.arange(row_count)
    allowed = (segment[:, None] == segment[None, :]) & (position[None, :] <= position[:, None])
    scores = jnp.einsum(
        "qhd,khd->hqk", query_part, key_part, preferred_element_type=jnp.float32
    ) * head_size ** (-0.5)
    weights = jnp.where(allowed[None], jax.nn.silu(scores), 0.0).astype(jnp.bfloat16)
    attended = jnp.einsum(
        "hqk,khd->qhd", weights, value_part, preferred_element_type=jnp.float32
    ).reshape(row_count, width)
    gated = (normalize(attended) * gate_part.astype(jnp.float32)).astype(jnp.bfloat16)
    result = embedded.astype(jnp.float32) + jnp.dot(
        gated, w_out, preferred_element_type=jnp.float32
    )
    return result.astype(jnp.bfloat16)


def on_device(table, owner, row_in_shard, segment, w_in, w_out, cotangent):
    shards = lax.axis_size("table")
    row_count = owner.shape[1]
    capacity = 2 * row_count // shards
    slot_total = shards * capacity
    vocab_rows = table.shape[0]
    target = owner[0, :, 0]
    local_row = row_in_shard[0]
    chosen = target[:, None] == jnp.arange(shards)[None, :]
    rank_all = jnp.cumsum(chosen.astype(jnp.int32), axis=0) - 1
    rank_own = jnp.sum(jnp.where(chosen, rank_all, 0), axis=1)
    slot_index = target * capacity + rank_own
    slot_match = slot_index[None, :] == jnp.arange(slot_total)[:, None]
    filled = jnp.any(slot_match, axis=1)
    source_row = jnp.sum(jnp.where(slot_match, jnp.arange(row_count)[None, :], 0), axis=1)
    request = jnp.where(filled, jnp.take(local_row, source_row), -1).reshape(shards, capacity)
    asked_rows = lax.all_to_all(request, "table", split_axis=0, concat_axis=0, tiled=True)
    is_valid = asked_rows >= 0
    found_rows = jnp.take(table, jnp.maximum(asked_rows, 0).reshape(-1), axis=0).reshape(
        shards, capacity, -1
    )
    found_rows = jnp.where(is_valid[..., None], found_rows, jnp.zeros((), table.dtype))
    returned = lax.all_to_all(found_rows, "table", split_axis=0, concat_axis=0, tiled=True)
    embedded = jnp.take(returned.reshape(slot_total, -1), slot_index, axis=0)
    seg_rows = segment[0]

    def local_layer(emb_in, weight_in, weight_out):
        return hstu_layer(emb_in, weight_in, weight_out, seg_rows)

    layer_rows, pullback = jax.vjp(local_layer, embedded, w_in, w_out)
    d_emb, d_in, d_out = pullback(cotangent[0])
    sent_grads = jnp.where(
        filled[:, None], jnp.take(d_emb, source_row, axis=0), jnp.zeros((), d_emb.dtype)
    )
    arrived = lax.all_to_all(
        sent_grads.reshape(shards, capacity, -1), "table", split_axis=0, concat_axis=0, tiled=True
    )
    flat_grads = arrived.reshape(slot_total, -1)
    table_ids = jnp.where(is_valid, asked_rows, vocab_rows).reshape(-1)
    all_rows, all_ids = (
        lax.all_gather(flat_grads, "dp", axis=0, tiled=True),
        lax.all_gather(table_ids, "dp", axis=0, tiled=True),
    )
    grad_table = jax.ops.segment_sum(
        all_rows.astype(jnp.float32), all_ids, num_segments=vocab_rows + 1
    )[:vocab_rows]
    share_in, share_out = (
        lax.psum_scatter(
            d_in.astype(jnp.float32).astype(jnp.bfloat16), "dp", scatter_dimension=1, tiled=True
        ).astype(jnp.float32),
        lax.psum_scatter(
            d_out.astype(jnp.float32).astype(jnp.bfloat16), "dp", scatter_dimension=0, tiled=True
        ).astype(jnp.float32),
    )
    grad_w_in, grad_w_out = lax.psum((share_in, share_out), "table")
    return (layer_rows[None], grad_table, grad_w_in, grad_w_out)


def solution(mesh):
    placed = (
        P("table", None),
        P(("table", "dp"), None, None),
        P(("table", "dp"), None),
        P(("table", "dp"), None),
        P(),
        P(),
        P(("table", "dp"), None, None),
    )
    return jax.shard_map(
        on_device,
        mesh=mesh,
        in_specs=placed,
        out_specs=(P(("table", "dp"), None, None), P("table", None), P(None, "dp"), P("dp", None)),
        check_vma=False,
    )
```

profile of v0, /device:TPU:6, one launch (start us, length us, event | category | flops | bytes accessed | tf_op | source)
XLA Modules:
  0.0 500.3 jit_solution(4746086050400691142)
XLA Ops:
  10.9 3.6 gather_fusion
  14.6 33.0 %all_to_all.19 = s32[64,1,8]{2,1,0:T(1,128)S(1)} all-to-all(s32[64,1,8]{2,1,0:T(1,128)S(1)} %bitcast.116), channel_id=1, replica_groups=mesh['table'=64,'dp'=8] {'table'}, dimensions={0} | all-to-all | bytes 4096 | tf_op jit(solution)/shard_map/all_to_all | solution.py:62
  47.8 2.0 gather_fusion.1
  50.8 4.6 all-to-all-start.1
  55.6 30.4 %all-to-all-done.1 = bf16[64,8,512]{2,1,0:T(8,128)(2,1)S(1)} async-done(((bf16[64,8,512]{2,1,0:T(8,128)(2,1)}), bf16[64,8,512]{2,1,0:T(8,128)(2,1)S(1)}, u32[]{:S(2)}, u32[]{:S(2)}) %all-to-all-start.1) | async-done | bytes 524320 | tf_op jit(solution)/shard_map/all_to_all | solution.py:68
  87.7 2.2 multiply_convert_fusion
  91.4 2.1 select_convert_fusion
  96.3 2.0 fusion.40
  98.6 2.3 fusion.43
  100.9 3.0 fusion.6
  103.9 1.8 copy.54
  105.8 2.1 convolution_convert_fusion.2
  108.2 1.9 fusion.45
  110.1 1.8 copy.52
  111.9 2.1 fusion.44
  115.1 4.5 convolution_convert_fusion
  120.7 3.3 fusion.18
  124.5 2.0 gather_fusion.3
  126.7 37.3 %all_to_all.20 = bf16[64,8,512]{2,1,0:T(8,128)(2,1)} all-to-all(bf16[64,8,512]{2,1,0:T(8,128)(2,1)S(1)} %fusion.19), channel_id=1, replica_groups=mesh['table'=64,'dp'=8] {'table'}, dimensions={0} | all-to-all | bytes 1048576 | tf_op jit(solution)/shard_map/all_to_all | solution.py:80
  165.4 11.1 %all-gather = s32[8,1,512]{2,1,0:T(1,128)S(1)} all-gather(s32[1,1,512]{2,1,0:T(1,128)S(1)} %bitcast.123), channel_id=1, replica_groups=mesh['table'=64,'dp'=8] {'dp'}, dimensions={0}, use_global_device_ids=true | all-gather | bytes 18432 | tf_op jit(solution)/shard_map/all_gather | solution.py:87
  176.4 2.1 fusion.10
  178.5 1.7 reduce-scatter.3.cloned.1.call-done
  180.2 286.9 %all-reduce.6 = (f32[512,256]{1,0:T(8,128)}, f32[64,512]{1,0:T(8,128)}) all-reduce(bf16[512,256]{1,0:T(8,128)(2,1)} %reduce-scatter.3.cloned.1.call-done, bf16[64,512]{1,0:T(8,128)(2,1)} %reduce-scatter.5.cloned.1.call-done), channel_id=1, replica_groups=mesh['table'=64,'dp'=8] {'table'}, use_global_device_ids=true, to_apply=%region_15.16 | all-reduce | flops 163840 | bytes 983040 | tf_op jit(solution)/shard_map/psum | solution.py:100
  467.1 25.7 %scatter_custom_fusion = f32[385,512]{1,0:T(8,128)S(1)} fusion(s32[4096]{0:T(1024)S(1)} %bitcast.121, bf16[4096,512]{1,0:T(8,128)(2,1)} %all-gather.3.cloned.1.call-done, f32[]{:T(128)} %constant.95.clone.1), kind=kCustom, calls=%fused_computation.5 | custom fusion | flops 4194304 | bytes 4982788 | tf_op jit(solution)/shard_map/scatter-add | solution.py:89
  (93 shorter events, 16.7 us)
Async XLA Ops:
  7.2 80.5 %copy-start = (bf16[512,2048]{1,0:T(8,128)(2,1)S(1)}, bf16[512,2048]{1,0:T(8,128)(2,1)}, u32[]{:S(2)}) copy-start(bf16[512,2048]{1,0:T(8,128)(2,1)} %param.11) | copy-start | bytes 6291460
  7.2 40.6 %copy-start.1 = (bf16[384,512]{1,0:T(8,128)(2,1)S(1)}, bf16[384,512]{1,0:T(8,128)(2,1)}, u32[]{:S(2)}) copy-start(bf16[384,512]{1,0:T(8,128)(2,1)} %param.7) | copy-start | bytes 1179652
  49.7 5.7 %copy-start.13 = (s32[1,256,1]{1,2,0:T(1,128)S(1)}, s32[1,256,1]{1,2,0:T(1,128)}, u32[]{:S(2)}) copy-start(s32[1,256,1]{1,2,0:T(1,128)} %param.8) | copy-start | bytes 3076
  49.7 5.7 %copy-start.14 = (s32[1,256]{1,0:T(1,128)S(1)}, s32[1,256]{1,0:T(1,128)}, u32[]{:S(2)}) copy-start(s32[1,256]{1,0:T(1,128)} %param.10) | copy-start | bytes 3076
  50.8 35.3 %all-to-all-start.1 = ((bf16[64,8,512]{2,1,0:T(8,128)(2,1)}), bf16[64,8,512]{2,1,0:T(8,128)(2,1)S(1)}, u32[]{:S(2)}, u32[]{:S(2)}) async-start(bf16[64,8,512]{2,1,0:T(8,128)(2,1)} %fusion.22), calls=%async_computation.1 | async-start | bytes 1048576 | tf_op jit(solution)/shard_map/all_to_all | solution.py:68
  55.4 123.1 %reduce-scatter.5.cloned.1.call-start = ((), (), s32[]{:S(2)}) async-start(), calls=%async_computation.7 | async-start | bytes 589824 | tf_op jit(solution)/shard_map/reduce_scatter | solution.py:96
  89.9 1.0 copy-start.4
  91.0 2.4 copy-start.7
  91.2 2.2 copy-start.8
  91.3 2.1 copy-start.5
  93.4 1.0 copy-start.2
  98.6 2.3 copy-start.9
  107.9 72.2 %reduce-scatter.3.cloned.1.call-start = ((), (), s32[]{:S(2)}) async-start(), calls=%async_computation.6 | async-start | bytes 2359296 | tf_op jit(solution)/shard_map/reduce_scatter | solution.py:93
  119.5 1.0 copy-start.10
  119.6 1.0 copy-start.11
  119.6 1.1 copy-start.12
  119.6 347.5 %all-gather.3.cloned.1.call-start = ((), (), s32[]{:S(2)}) async-start(), calls=%async_computation.5 | async-start | bytes 4718592 | tf_op jit(solution)/shard_map/all_gather | solution.py:86
  120.7 3.6 copy-start.3
  126.5 49.9 %copy-start.6 = (bf16[256,512]{1,0:T(8,128)(2,1)S(1)}, bf16[256,512]{1,0:T(8,128)(2,1)}, u32[]{:S(2)}) copy-start(bf16[256,512]{1,0:T(8,128)(2,1)} %get-tuple-element.10) | copy-start | bytes 786436
Sparse Core Ops, SparseCore 0:
  108.1 28.4 reduce-scatter.4
  139.4 40.7 reduce-scatter.2
  182.3 39.6 all-gather.2
where the time goes:
time: 501 us; the launch traced here: 500 us
  blocking collectives  368 us (73%)
  other arithmetic  34.4 us (7%)
  waiting for transfers between devices  32.2 us (6%)
  matrix products  27.6 us (6%)
  local copies, waits for them, and re-layouts  18.7 us (4%)
  between operations  14.2 us (3%)
    psum x1, blocking collectives, on_device(): grad_w_in, grad_w_out = lax.psum((share_in, share_out), 'table')  287 us
    all_to_all x1, blocking collectives, on_device(): lax.all_to_all(sent_grads.reshape(shards, capacity, -1), 'table', split_a...  37.3 us
    all_to_all x1, blocking collectives, on_device(): lax.all_to_all(request, 'table', split_axis=0, concat_axis=0, tiled=True)  33 us
    all_to_all x1, waiting for transfers between devices, on_device(): lax.all_to_all(found_rows, 'table', split_axis=0, concat_axis=0, tiled=True)  30.4 us
    scatter-add x1, other arithmetic, on_device(): jax.ops.segment_sum(all_rows.astype(jnp.float32), all_ids, num_segments=v...  25.7 us
    all_gather x1, blocking collectives, on_device(): lax.all_gather(table_ids, 'dp', axis=0, tiled=True)  11.1 us
  transfers between devices with their start and end apart: 4, of which 2 were waited for; matrix products, arithmetic and copies ran while one was open for 4% of the time, Pallas kernels for 0%

commit v1 on v0

v1 whole, which is shorter than its diff:
```python
import jax
import jax.numpy as jnp
from jax import lax
from jax.experimental import pallas as pl
from jax.experimental.pallas import tpu as pltpu
from jax.sharding import Mesh, PartitionSpec as P

HEADS = 8
EPS = 1e-05
CAP = 8
BF = jnp.bfloat16
F32 = jnp.float32
TABLE = ("y", "z")
DP = ("x", "c")
ALL = ("y", "z", "x", "c")


def iota(shape, dim):
    return lax.broadcasted_iota(jnp.int32, shape, dim)


def dot(a, b, dims=((1,), (0,))):
    return lax.dot_general(a, b, (dims, ((), ())), preferred_element_type=F32)


def plan_kernel(owner_ref, row_ref, request_ref, slot_ref):
    rows = owner_ref.shape[1]
    shards = request_ref.shape[0]
    own = owner_ref[...].astype(F32)
    row = row_ref[...].astype(F32)
    first = iota((rows, rows), 0)
    second = iota((rows, rows), 1)
    own_col = jnp.sum(jnp.where(first == second, own, 0.0), axis=1, keepdims=True)
    earlier = (own_col == own) & (first < second)
    rank = jnp.sum(jnp.where(earlier, 1.0, 0.0), axis=0, keepdims=True)
    slot_ref[...] = (own * CAP + rank).astype(jnp.int32)
    mine = jnp.where(iota((shards, rows), 0).astype(F32) == own, row + 1.0, 0.0)
    lane = iota((shards, 128), 1)
    request = jnp.full((shards, 128), -1.0, F32)
    for k in range(CAP):
        found = jnp.sum(jnp.where(rank == float(k), mine, 0.0), axis=1, keepdims=True)
        request = jnp.where(lane == k, found - 1.0, request)
    request_ref[...] = request.astype(jnp.int32)


def plan(owner, row, shards):
    return pl.pallas_call(
        plan_kernel,
        out_shape=(
            jax.ShapeDtypeStruct((shards, 128), jnp.int32),
            jax.ShapeDtypeStruct(owner.shape, jnp.int32),
        ),
        name="plan",
    )(owner, row)


def chosen_rows(asked_ref, vocab_rows):
    shards = asked_ref.shape[0]
    slots = shards * CAP
    asked = asked_ref[...].astype(F32)
    spread = jnp.broadcast_to(asked[:, None, :], (shards, CAP, 128)).reshape(slots, 128)
    keep = iota((slots, 128), 1) == (iota((slots, 128), 0) % CAP)
    column = jnp.sum(jnp.where(keep, spread, 0.0), axis=1, keepdims=True)
    return jnp.where(column == iota((slots, vocab_rows), 1).astype(F32), 1.0, 0.0).astype(BF)


def serve_kernel(asked_ref, table_ref, found_ref):
    found_ref[...] = dot(chosen_rows(asked_ref, table_ref.shape[0]), table_ref[...]).astype(BF)


def serve(asked, table):
    return pl.pallas_call(
        serve_kernel,
        out_shape=jax.ShapeDtypeStruct((asked.shape[0] * CAP, table.shape[1]), BF),
        name="serve",
    )(asked, table)


def collect_kernel(asked_ref, grads_ref, sum_ref):
    chosen = chosen_rows(asked_ref, sum_ref.shape[0])
    sum_ref[...] = dot(chosen, grads_ref[...], ((0,), (0,))).astype(sum_ref.dtype)


def collect(asked, grads, vocab_rows):
    return pl.pallas_call(
        collect_kernel,
        out_shape=jax.ShapeDtypeStruct((vocab_rows, grads.shape[1]), BF),
        name="collect",
    )(asked, grads)


def layer_kernel(
    slot_ref, segment_ref, returned_ref, w_in_ref, w_out_ref, cot_ref,
    out_ref, d_in_ref, d_out_ref, sent_ref,
    mixed, slope, attended, d_mixed,
):
    rows, width = cot_ref.shape
    slots = returned_ref.shape[0]
    head = width // HEADS
    pair = 2 * head
    scale = head ** (-0.5)
    match = jnp.where(iota((slots, rows), 0) == slot_ref[...], 1.0, 0.0).astype(BF)
    embedded = dot(match, returned_ref[...], ((0,), (0,)))
    average = jnp.mean(embedded, axis=-1, keepdims=True)
    centred = embedded - average
    inverse = lax.rsqrt(jnp.mean(centred * centred, axis=-1, keepdims=True) + EPS)
    hat = centred * inverse
    normed = hat.astype(BF)
    for part in range(4):
        span = slice(part * width, (part + 1) * width)
        pre = dot(normed, w_in_ref[:, span])
        sig = jax.nn.sigmoid(pre)
        value = pre * sig
        mixed[:, span] = value.astype(BF)
        slope[:, span] = sig + value * (1.0 - sig)
    seg = segment_ref[...].astype(F32)
    first = iota((rows, rows), 0)
    second = iota((rows, rows), 1)
    seg_col = jnp.sum(jnp.where(first == second, seg, 0.0), axis=1, keepdims=True)
    allowed = (seg_col == seg) & (second <= first)
    low = iota((rows, pair), 1) < head
    zero = jnp.zeros((rows, pair), BF)

    def parts(block):
        return jnp.where(low, block, zero), jnp.where(low, zero, block)

    def at(part, p):
        return slice(part * width + p * pair, part * width + (p + 1) * pair)

    def weigh(q, k):
        score = dot(q, k, ((1,), (1,))) * scale
        sig = jax.nn.sigmoid(score)
        return score, sig

    for p in range(HEADS // 2):
        values, keys = mixed[:, at(1, p)], mixed[:, at(3, p)]
        halves = []
        for q in parts(mixed[:, at(2, p)]):
            score, sig = weigh(q, keys)
            weights = jnp.where(allowed, score * sig, 0.0).astype(BF)
            halves.append(dot(weights, values))
        attended[:, p * pair : (p + 1) * pair] = jnp.where(low, halves[0], halves[1])
    att = attended[...]
    centred = att - jnp.mean(att, axis=-1, keepdims=True)
    inverse_a = lax.rsqrt(jnp.mean(centred * centred, axis=-1, keepdims=True) + EPS)
    hat_a = centred * inverse_a
    gate = mixed[:, :width].astype(F32)
    gated = (hat_a * gate).astype(BF)
    out_ref[...] = (embedded + dot(gated, w_out_ref[...])).astype(BF)
    cot = cot_ref[...]
    d_out_ref[...] = dot(gated, cot, ((0,), (0,))).astype(BF)
    d_gated = dot(cot, w_out_ref[...], ((1,), (1,))).astype(BF).astype(F32)
    d_mixed[:, :width] = ((d_gated * hat_a).astype(BF).astype(F32) * slope[:, :width]).astype(BF)
    d_hat = d_gated * gate
    d_att = inverse_a * (
        d_hat
        - jnp.mean(d_hat, axis=-1, keepdims=True)
        - hat_a * jnp.mean(d_hat * hat_a, axis=-1, keepdims=True)
    )
    attended[...] = d_att
    for p in range(HEADS // 2):
        values, keys, queries = mixed[:, at(1, p)], mixed[:, at(3, p)], mixed[:, at(2, p)]
        d_pair = attended[:, p * pair : (p + 1) * pair].astype(BF)
        found = []
        for q, d_half in zip(parts(queries), parts(d_pair)):
            score, sig = weigh(q, keys)
            value = score * sig
            weights = jnp.where(allowed, value, 0.0).astype(BF)
            d_weights = dot(d_half, values, ((1,), (1,))).astype(BF).astype(F32)
            d_score = jnp.where(
                allowed, d_weights * (sig + value * (1.0 - sig)) * scale, 0.0
            ).astype(BF)
            found.append(
                (
                    dot(weights, d_pair, ((0,), (0,))),
                    dot(d_score, keys),
                    dot(d_score, queries, ((0,), (0,))),
                )
            )
        for part in range(3):
            span = at(part + 1, p)
            whole = jnp.where(low, found[0][part], found[1][part]).astype(BF).astype(F32)
            d_mixed[:, span] = (whole * slope[:, span]).astype(BF)
    d_all = d_mixed[...]
    d_in_ref[...] = dot(normed, d_all, ((0,), (0,))).astype(BF)
    d_normed = dot(d_all, w_in_ref[...], ((1,), (1,))).astype(BF).astype(F32)
    d_emb = inverse * (
        d_normed
        - jnp.mean(d_normed, axis=-1, keepdims=True)
        - hat * jnp.mean(d_normed * hat, axis=-1, keepdims=True)
    )
    d_emb = (cot.astype(F32) + d_emb).astype(BF)
    sent_ref[...] = dot(match, d_emb).astype(BF)


def layer(slot, segment, returned, w_in, w_out, cot):
    rows, width = cot.shape
    return pl.pallas_call(
        layer_kernel,
        out_shape=(
            jax.ShapeDtypeStruct((rows, width), BF),
            jax.ShapeDtypeStruct(w_in.shape, BF),
            jax.ShapeDtypeStruct(w_out.shape, BF),
            jax.ShapeDtypeStruct(returned.shape, BF),
        ),
        scratch_shapes=[
            pltpu.VMEM((rows, 4 * width), BF),
            pltpu.VMEM((rows, 4 * width), F32),
            pltpu.VMEM((rows, width), F32),
            pltpu.VMEM((rows, 4 * width), BF),
        ],
        name="layer",
    )(slot, segment, returned, w_in, w_out, cot)


def share_sum_kernel(own_ref, a_ref, b_ref, c_ref, sum_ref):
    total = own_ref[...].astype(F32) + a_ref[...].astype(F32)
    total = total + b_ref[...].astype(F32) + c_ref[...].astype(F32)
    sum_ref[...] = total.astype(sum_ref.dtype)


def shift(x, axis, by, size):
    return lax.ppermute(x, axis, [(i, (i + by) % size) for i in range(size)])


def exchange(x, axes):
    return lax.all_to_all(x, axes, split_axis=0, concat_axis=0, tiled=True)


def part_of(x, index):
    return lax.dynamic_index_in_dim(x, index, 0, keepdims=False)


def on_device(table, owner, row_in_shard, segment, w_in, w_out, cotangent):
    shards = 64
    vocab_rows, width = table.shape
    rows = owner.shape[1]
    x, c = lax.axis_index("x"), lax.axis_index("c")
    request, slot = plan(owner.reshape(1, rows), row_in_shard, shards)
    asked = exchange(request.reshape(shards, 1, 128), TABLE).reshape(shards, 128)
    found = serve(asked, table)
    returned = exchange(found.reshape(shards, CAP, width), TABLE).reshape(shards * CAP, width)
    out, d_in, d_out, sent = layer(slot, segment, returned, w_in, w_out, cotangent[0])
    blocks = jnp.concatenate(
        [
            d_in.reshape(width, 4, 2, 256).transpose(1, 2, 0, 3).reshape(4, 2, 256, 512),
            d_out.reshape(4, 2, 64, 512),
        ],
        axis=2,
    )
    mine = lax.dynamic_index_in_dim(blocks, c, 1, keepdims=False)
    other = lax.dynamic_index_in_dim(blocks, 1 - c, 1, keepdims=False)
    other = lax.ppermute(other, "c", [(0, 1), (1, 0)])
    halves = (mine.astype(F32) + other.astype(F32)).astype(BF)
    arrived = exchange(sent.reshape(shards, CAP, width), TABLE).reshape(shards * CAP, width)
    pieces = [part_of(halves, x)] + [
        shift(part_of(halves, (x + k) % 4), "x", k, 4) for k in (1, 2, 3)
    ]
    share = sum(p.astype(F32) for p in pieces)
    share = exchange(share.astype(BF).reshape(shards, 2560), TABLE)
    share = jnp.sum(share.astype(F32), axis=0).astype(BF)
    share = exchange(jnp.broadcast_to(share[None], (shards, 2560)), TABLE).astype(F32)
    share = share.reshape(320, 512)
    part = collect(asked, arrived, vocab_rows)
    part = part.reshape(2, 192, width)
    other = lax.ppermute(part_of(part, 1 - c), "c", [(0, 1), (1, 0)])
    half = (part_of(part, c).astype(F32) + other.astype(F32)).astype(BF)
    halves = [half] + [shift(half, "x", k, 4) for k in (1, 2, 3)]
    half = sum(h.astype(F32) for h in halves)
    other = lax.ppermute(half, "c", [(0, 1), (1, 0)])
    grad_table = jnp.where(c == 0, jnp.concatenate([half, other]), jnp.concatenate([other, half]))
    return out[None], grad_table, share[:256].reshape(512, 256), share[256:]


def solution(mesh):
    devices = mesh.devices
    grid = Mesh(devices.reshape(4, 16, 4, 2), ALL)
    placed = (
        P(TABLE, None),
        P(ALL, None, None),
        P(ALL, None),
        P(ALL, None),
        P(),
        P(),
        P(ALL, None, None),
    )
    return jax.shard_map(
        on_device,
        mesh=grid,
        in_specs=placed,
        out_specs=(P(ALL, None, None), P(TABLE, None), P(None, DP), P(DP, None)),
        check_vma=False,
    )
```

time: 501 us -> 208 us (0.42)
  blocking collectives: 368 us -> 33.1 us
  starting transfers between devices: 4.94 us -> 53.1 us
  waiting for transfers between devices: 32.2 us -> 77 us
  matrix products: 27.6 us -> 0 us
  other arithmetic: 34.4 us -> 11.7 us
  Pallas kernels: 0 us -> 16.1 us
  between operations: 14.2 us -> 0.96 us
    psum x1 -> x0, blocking collectives: 287 us -> none  [on_device(): grad_w_in, grad_w_out = lax.psum((share_in, share_out), 'table')]
    all_to_all x2 -> x1, blocking collectives: 70.2 us -> 33.1 us  [exchange(): return lax.all_to_all(x, axes, split_axis=0, concat_axis=0, tiled=True)]
    dot_general x12 -> x0, matrix products: 27.6 us -> none  [the longest x3 9.9 us: hstu_layer(): jnp.dot(normed, w_in, preferred_element_type=jnp.float32)]
    scatter-add x1 -> x0, other arithmetic: 25.7 us -> none  [on_device(): jax.ops.segment_sum(all_rows.astype(jnp.float32), all_ids, num_segments=v...]
    all_to_all x1 -> x4, waiting for transfers between devices: 30.4 us -> 56.1 us  [exchange(): return lax.all_to_all(x, axes, split_axis=0, concat_axis=0, tiled=True)]
    ppermute x0 -> x9, starting transfers between devices: none -> 24.3 us  [the longest x6 18.4 us: shift(): return lax.ppermute(x, axis, [(i, (i + by) % size) for i in range(size)])]
    all_to_all x1 -> x4, starting transfers between devices: 4.63 us -> 28.9 us  [exchange(): return lax.all_to_all(x, axes, split_axis=0, concat_axis=0, tiled=True)]
    ppermute x0 -> x9, waiting for transfers between devices: none -> 20.9 us  [the longest x6 19.2 us: shift(): return lax.ppermute(x, axis, [(i, (i + by) % size) for i in range(size)])]
  transfers between devices with their start and end apart: 4 -> 13, of which waited for: 2 -> 10; matrix products, arithmetic and copies ran while one was open for 4% -> 6% of each run, Pallas kernels for 0% -> 1%
where the time goes in v1:
time: 208 us; the launch traced here: 207 us
  waiting for transfers between devices  77 us (37%)
  starting transfers between devices  53.1 us (26%)
  blocking collectives  33.1 us (16%)
  Pallas kernels  16.1 us (8%)
  local copies, waits for them, and re-layouts  14.5 us (7%)
  other arithmetic  11.7 us (6%)
    all_to_all x4, waiting for transfers between devices, exchange(): return lax.all_to_all(x, axes, split_axis=0, concat_axis=0, tiled=True)  56.1 us
    all_to_all x1, blocking collectives, exchange(): return lax.all_to_all(x, axes, split_axis=0, concat_axis=0, tiled=True)  33.1 us
    all_to_all x4, starting transfers between devices, exchange(): return lax.all_to_all(x, axes, split_axis=0, concat_axis=0, tiled=True)  28.9 us
    ppermute x6, waiting for transfers between devices, shift(): return lax.ppermute(x, axis, [(i, (i + by) % size) for i in range(size)])  19.2 us
    ppermute x6, starting transfers between devices, shift(): return lax.ppermute(x, axis, [(i, (i + by) % size) for i in range(size)])  18.4 us
    pallas_call x1, Pallas kernels, layer(): pl.pallas_call(layer_kernel, out_shape=(jax.ShapeDtypeStruct((rows, width...  9.9 us
    reshape x3, local copies, waits for them, and re-layouts, on_device(): d_in.reshape(width, 4, 2, 256).transpose(1, 2, 0, 3).reshape(4, 2, 256, 512)  7.76 us
  transfers between devices with their start and end apart: 13, of which 10 were waited for; matrix products, arithmetic and copies ran while one was open for 6% of the time, Pallas kernels for 1%

profile of v1, /device:TPU:6, one launch (start us, length us, event | category | flops | bytes accessed | tf_op | source)
XLA Modules:
  0.0 206.5 jit_solution(7035286258957450852)
XLA Ops:
  2.2 33.1 %all_to_all.31 = s32[64,1,128]{2,1,0:T(1,128)} all-to-all(s32[64,1,128]{2,1,0:T(1,128)} %bitcast.49), channel_id=1, replica_groups=mesh['y'=4,'z'=16,'x'=4,'c'=2] {'y','z'}, dimensions={0} | all-to-all | bytes 65536 | tf_op jit(solution)/shard_map/all_to_all | solution.py:227
  35.3 2.3 %serve.1 = bf16[512,512]{1,0:T(8,128)(2,1)} custom-call(s32[64,128]{1,0:T(8,128)} %bitcast.46, bf16[384,512]{1,0:T(8,128)(2,1)} %table_ref.1), custom_call_target="tpu_custom_call" | custom-call | tf_op jit(solution)/shard_map/serve/pallas_call | solution.py:72
  37.6 4.6 %all-to-all-start.1 = ((bf16[64,8,512]{2,1,0:T(8,128)(2,1)}), bf16[64,8,512]{2,1,0:T(8,128)(2,1)S(1)}, u32[]{:S(2)}, u32[]{:S(2)}) async-start(bf16[64,8,512]{2,1,0:T(8,128)(2,1)} %bitcast.40), calls=%async_computation.1 | async-start | bytes 1048576 | tf_op jit(solution)/shard_map/all_to_all | solution.py:227
  42.2 30.8 %all-to-all-done.1 = bf16[64,8,512]{2,1,0:T(8,128)(2,1)S(1)} async-done(((bf16[64,8,512]{2,1,0:T(8,128)(2,1)}), bf16[64,8,512]{2,1,0:T(8,128)(2,1)S(1)}, u32[]{:S(2)}, u32[]{:S(2)}) %all-to-all-start.1) | async-done | bytes 524320 | tf_op jit(solution)/shard_map/all_to_all | solution.py:227
  73.8 9.9 %layer.1 = (bf16[256,512]{1,0:T(8,128)(2,1)}, bf16[512,2048]{1,0:T(8,128)(2,1)}, bf16[512,512]{1,0:T(8,128)(2,1)}, bf16[512,512]{1,0:T(8,128)(2,1)}) custom-call(s32[1,256]{1,0:T(1,128)} %get-tuple-element.10.slot_ref, s32[1,256]{1,0:T(1,128)} %segment_ref.1, bf16[512,512]{1,0:T(8,128)(2,1)} %bitcast.41, bf16[512,2048]{1,0:T(8,128)(2,1)} %w_in_ref.1, ...), custom_call_target="tpu_custom_call" | custom-call | tf_op jit(solution)/shard_map/layer/pallas_call | solution.py:198
  83.7 3.3 %reshape.72 = bf16[512,4,2,256]{3,2,1,0:T(2,128)(2,1)S(1)} reshape(bf16[512,2048]{1,0:T(8,128)(2,1)} %get-tuple-element.14) | data formatting | bytes 4194304 | tf_op jit(solution)/shard_map/reshape | solution.py:246
  88.7 2.7 %reshape.73 = bf16[4,2,256,512]{3,2,1,0:T(8,128)(2,1)S(1)} reshape(bf16[4,2,512,256]{3,2,1,0:T(8,128)(2,1)} %bitcast.39) | data formatting | bytes 4194304 | tf_op jit(solution)/shard_map/reshape | solution.py:246
  94.6 6.8 %all-to-all-start.2 = ((bf16[64,8,512]{2,1,0:T(8,128)(2,1)}), bf16[64,8,512]{2,1,0:T(8,128)(2,1)}, u32[]{:S(2)}, u32[]{:S(2)}) async-start(bf16[64,8,512]{2,1,0:T(8,128)(2,1)} %bitcast.8), calls=%async_computation.2 | async-start | bytes 1048576 | tf_op jit(solution)/shard_map/all_to_all | solution.py:227
  103.2 2.4 %collective-permute-start.6 = (bf16[320,512]{1,0:T(8,128)(2,1)S(1)}, bf16[320,512]{1,0:T(8,128)(2,1)S(1)}, u32[]{:S(2)}, u32[]{:S(2)}) collective-permute-start(bf16[320,512]{1,0:T(8,128)(2,1)S(1)} %get-tuple-element.16), channel_id=1, source_target_pairs={{0,2},{2,4},{4,6},{6,0},{1,3},{3,5},{5,7},{7,1},{8,10},{10,12},{12... | collective-permute-start | bytes 983048 | tf_op jit(solution)/shard_map/ppermute | solution.py:223
  105.6 4.3 %collective-permute-start.7 = (bf16[320,512]{1,0:T(8,128)(2,1)S(1)}, bf16[320,512]{1,0:T(8,128)(2,1)S(1)}, u32[]{:S(2)}, u32[]{:S(2)}) collective-permute-start(bf16[320,512]{1,0:T(8,128)(2,1)S(1)} %get-tuple-element.18), channel_id=1, source_target_pairs={{0,4},{2,6},{4,0},{6,2},{1,5},{3,7},{5,1},{7,3},{8,12},{10,14},{12... | collective-permute-start | bytes 983048 | tf_op jit(solution)/shard_map/ppermute | solution.py:223
  112.1 3.6 %collective-permute-done.6 = bf16[320,512]{1,0:T(8,128)(2,1)S(1)} collective-permute-done((bf16[320,512]{1,0:T(8,128)(2,1)S(1)}, bf16[320,512]{1,0:T(8,128)(2,1)S(1)}, u32[]{:S(2)}, u32[]{:S(2)}) %collective-permute-start.6) | collective-permute-done | bytes 327712 | tf_op jit(solution)/shard_map/ppermute | solution.py:223
  115.7 3.9 %collective-permute-done.7 = bf16[320,512]{1,0:T(8,128)(2,1)S(1)} collective-permute-done((bf16[320,512]{1,0:T(8,128)(2,1)S(1)}, bf16[320,512]{1,0:T(8,128)(2,1)S(1)}, u32[]{:S(2)}, u32[]{:S(2)}) %collective-permute-start.7) | collective-permute-done | bytes 327712 | tf_op jit(solution)/shard_map/ppermute | solution.py:223
  119.6 5.9 %collective-permute-done.8 = bf16[320,512]{1,0:T(8,128)(2,1)S(1)} collective-permute-done((bf16[320,512]{1,0:T(8,128)(2,1)S(1)}, bf16[320,512]{1,0:T(8,128)(2,1)S(1)}, u32[]{:S(2)}, u32[]{:S(2)}) %collective-permute-start.8) | collective-permute-done | bytes 327712 | tf_op jit(solution)/shard_map/ppermute | solution.py:223
  126.5 2.6 %reduce.4 = bf16[64,2560]{1,0:T(8,128)(2,1)S(1)} reduce(bf16[64,1,2560]{2,1,0:T(2,128)(2,1)S(1)} %all_to_all.25, bf16[]{:T(256)} %broadcast.7), dimensions={1}, to_apply=%all_to_all.25.reduce_sub_computation | reduce | bytes 655362 | tf_op jit(solution)/shard_map/all_to_all | solution.py:227
  129.9 3.9 %all-to-all-done.2 = bf16[64,8,512]{2,1,0:T(8,128)(2,1)} async-done(((bf16[64,8,512]{2,1,0:T(8,128)(2,1)}), bf16[64,8,512]{2,1,0:T(8,128)(2,1)}, u32[]{:S(2)}, u32[]{:S(2)}) %all-to-all-start.2) | async-done | bytes 524320 | tf_op jit(solution)/shard_map/all_to_all | solution.py:227
  133.8 10.9 %all-to-all-start.3 = ((bf16[64,2,1280]{2,1,0:T(2,128)(2,1)}), bf16[64,2,1280]{2,1,0:T(2,128)(2,1)S(1)}, u32[]{:S(2)}, u32[]{:S(2)}) async-start(bf16[64,2,1280]{2,1,0:T(2,128)(2,1)} %reshape.81), calls=%async_computation.3 | async-start | bytes 655360 | tf_op jit(solution)/shard_map/all_to_all | solution.py:227
  144.7 2.3 %collect.1 = bf16[384,512]{1,0:T(8,128)(2,1)} custom-call(s32[64,128]{1,0:T(8,128)} %bitcast.47, bf16[512,512]{1,0:T(8,128)(2,1)} %bitcast.9.grads_ref), custom_call_target="tpu_custom_call" | custom-call | tf_op jit(solution)/shard_map/collect/pallas_call | solution.py:85
  150.0 18.5 %all-to-all-done.3 = bf16[64,2,1280]{2,1,0:T(2,128)(2,1)S(1)} async-done(((bf16[64,2,1280]{2,1,0:T(2,128)(2,1)}), bf16[64,2,1280]{2,1,0:T(2,128)(2,1)S(1)}, u32[]{:S(2)}, u32[]{:S(2)}) %all-to-all-start.3) | async-done | bytes 327712 | tf_op jit(solution)/shard_map/all_to_all | solution.py:227
  169.7 2.6 %reduce.5 = bf16[64,2560]{1,0:T(8,128)(2,1)S(1)} reduce(bf16[64,1,2560]{2,1,0:T(2,128)(2,1)S(1)} %broadcast_in_dim.10, bf16[]{:T(256)} %broadcast.7), dimensions={1}, to_apply=%broadcast_in_dim.10.reduce_sub_computation | reduce | bytes 655362 | tf_op jit(solution)/shard_map/broadcast_in_dim | solution.py:262
  173.1 6.5 %all-to-all-start.4 = ((bf16[64,2,1280]{2,1,0:T(2,128)(2,1)}), bf16[64,2,1280]{2,1,0:T(2,128)(2,1)S(1)}, u32[]{:S(2)}, u32[]{:S(2)}) async-start(bf16[64,2,1280]{2,1,0:T(2,128)(2,1)} %reshape.83), calls=%async_computation.4 | async-start | bytes 655360 | tf_op jit(solution)/shard_map/all_to_all | solution.py:227
  181.6 4.3 %collective-permute-start.2 = (bf16[192,512]{1,0:T(8,128)(2,1)S(1)}, bf16[192,512]{1,0:T(8,128)(2,1)S(1)}, u32[]{:S(2)}, u32[]{:S(2)}) collective-permute-start(bf16[192,512]{1,0:T(8,128)(2,1)S(1)} %fusion.8), channel_id=1, source_target_pairs={{0,4},{2,6},{4,0},{6,2},{1,5},{3,7},{5,1},{7,3},{8,12},{10,14},{12... | collective-permute-start | bytes 589832 | tf_op jit(solution)/shard_map/ppermute | solution.py:223
  186.0 3.3 %collective-permute-start.3 = (bf16[192,512]{1,0:T(8,128)(2,1)S(1)}, bf16[192,512]{1,0:T(8,128)(2,1)S(1)}, u32[]{:S(2)}, u32[]{:S(2)}) collective-permute-start(bf16[192,512]{1,0:T(8,128)(2,1)S(1)} %fusion.8), channel_id=1, source_target_pairs={{0,6},{2,0},{4,2},{6,4},{1,7},{3,1},{5,3},{7,5},{8,14},{10,8},{12,... | collective-permute-start | bytes 589832 | tf_op jit(solution)/shard_map/ppermute | solution.py:223
  191.0 4.0 %collective-permute-done.3 = bf16[192,512]{1,0:T(8,128)(2,1)S(1)} collective-permute-done((bf16[192,512]{1,0:T(8,128)(2,1)S(1)}, bf16[192,512]{1,0:T(8,128)(2,1)S(1)}, u32[]{:S(2)}, u32[]{:S(2)}) %collective-permute-start.3) | collective-permute-done | bytes 196640 | tf_op jit(solution)/shard_map/ppermute | solution.py:223
  199.7 3.0 %all-to-all-done.4 = bf16[64,2,1280]{2,1,0:T(2,128)(2,1)S(1)} async-done(((bf16[64,2,1280]{2,1,0:T(2,128)(2,1)}), bf16[64,2,1280]{2,1,0:T(2,128)(2,1)S(1)}, u32[]{:S(2)}, u32[]{:S(2)}) %all-to-all-start.4) | async-done | bytes 327712 | tf_op jit(solution)/shard_map/all_to_all | solution.py:227
  (39 shorter events, 30.0 us)
Async XLA Ops:
  37.6 35.4 %all-to-all-start.1 = ((bf16[64,8,512]{2,1,0:T(8,128)(2,1)}), bf16[64,8,512]{2,1,0:T(8,128)(2,1)S(1)}, u32[]{:S(2)}, u32[]{:S(2)}) async-start(bf16[64,8,512]{2,1,0:T(8,128)(2,1)} %bitcast.40), calls=%async_computation.1 | async-start | bytes 1048576 | tf_op jit(solution)/shard_map/all_to_all | solution.py:227
  73.0 0.8 copy-start
  88.7 2.7 %copy-start.1 = (bf16[512,512]{1,0:T(8,128)(2,1)S(1)}, bf16[512,512]{1,0:T(8,128)(2,1)}, u32[]{:S(2)}) copy-start(bf16[512,512]{1,0:T(8,128)(2,1)} %get-tuple-element.15) | copy-start | bytes 1572868
  92.6 8.8 %collective-permute-start.5 = (bf16[4,320,512]{2,1,0:T(8,128)(2,1)}, bf16[4,320,512]{2,1,0:T(8,128)(2,1)}, u32[]{:S(2)}, u32[]{:S(2)}) collective-permute-start(bf16[4,320,512]{2,1,0:T(8,128)(2,1)} %fusion.2), channel_id=1, source_target_pairs={{0,1},{1,0},{2,3},{3,2},{4,5},{5,4},{6,7},{7,6},{8,9},{9,8},{10,11... | collective-permute-start | bytes 3932168 | tf_op jit(solution)/shard_map/ppermute | solution.py:253
  94.6 39.2 %all-to-all-start.2 = ((bf16[64,8,512]{2,1,0:T(8,128)(2,1)}), bf16[64,8,512]{2,1,0:T(8,128)(2,1)}, u32[]{:S(2)}, u32[]{:S(2)}) async-start(bf16[64,8,512]{2,1,0:T(8,128)(2,1)} %bitcast.8), calls=%async_computation.2 | async-start | bytes 1048576 | tf_op jit(solution)/shard_map/all_to_all | solution.py:227
  103.2 12.5 %collective-permute-start.6 = (bf16[320,512]{1,0:T(8,128)(2,1)S(1)}, bf16[320,512]{1,0:T(8,128)(2,1)S(1)}, u32[]{:S(2)}, u32[]{:S(2)}) collective-permute-start(bf16[320,512]{1,0:T(8,128)(2,1)S(1)} %get-tuple-element.16), channel_id=1, source_target_pairs={{0,2},{2,4},{4,6},{6,0},{1,3},{3,5},{5,7},{7,1},{8,10},{10,12},{12... | collective-permute-start | bytes 983048 | tf_op jit(solution)/shard_map/ppermute | solution.py:223
  105.6 14.0 %collective-permute-start.7 = (bf16[320,512]{1,0:T(8,128)(2,1)S(1)}, bf16[320,512]{1,0:T(8,128)(2,1)S(1)}, u32[]{:S(2)}, u32[]{:S(2)}) collective-permute-start(bf16[320,512]{1,0:T(8,128)(2,1)S(1)} %get-tuple-element.18), channel_id=1, source_target_pairs={{0,4},{2,6},{4,0},{6,2},{1,5},{3,7},{5,1},{7,3},{8,12},{10,14},{12... | collective-permute-start | bytes 983048 | tf_op jit(solution)/shard_map/ppermute | solution.py:223
  110.0 15.6 %collective-permute-start.8 = (bf16[320,512]{1,0:T(8,128)(2,1)S(1)}, bf16[320,512]{1,0:T(8,128)(2,1)S(1)}, u32[]{:S(2)}, u32[]{:S(2)}) collective-permute-start(bf16[320,512]{1,0:T(8,128)(2,1)S(1)} %get-tuple-element.17), channel_id=1, source_target_pairs={{0,6},{2,0},{4,2},{6,4},{1,7},{3,1},{5,3},{7,5},{8,14},{10,8},{12,... | collective-permute-start | bytes 983048 | tf_op jit(solution)/shard_map/ppermute | solution.py:223
  133.8 34.7 %all-to-all-start.3 = ((bf16[64,2,1280]{2,1,0:T(2,128)(2,1)}), bf16[64,2,1280]{2,1,0:T(2,128)(2,1)S(1)}, u32[]{:S(2)}, u32[]{:S(2)}) async-start(bf16[64,2,1280]{2,1,0:T(2,128)(2,1)} %reshape.81), calls=%async_computation.3 | async-start | bytes 655360 | tf_op jit(solution)/shard_map/all_to_all | solution.py:227
  148.0 31.7 %copy-start.2 = (bf16[384,512]{1,0:T(8,128)(2,1)S(1)}, bf16[384,512]{1,0:T(8,128)(2,1)}, u32[]{:S(2)}) copy-start(bf16[384,512]{1,0:T(8,128)(2,1)} %collect.1) | copy-start | bytes 1179652
  148.0 31.6 %collective-permute-start = (bf16[192,512]{1,0:T(8,128)(2,1)S(1)}, bf16[192,512]{1,0:T(8,128)(2,1)S(1)}, u32[]{:S(2)}, u32[]{:S(2)}) collective-permute-start(bf16[192,512]{1,0:T(8,128)(2,1)S(1)} %dynamic-slice_bitcast_fusion.3), channel_id=1, source_target_pairs={{0,1},{1,0},{2,3},{3,2},{4,5},{5,4},{6,7},{7,6},{8,9},{9,8},{10,11... | collective-permute-start | bytes 589832 | tf_op jit(solution)/shard_map/ppermute | solution.py:266
  173.1 29.6 %all-to-all-start.4 = ((bf16[64,2,1280]{2,1,0:T(2,128)(2,1)}), bf16[64,2,1280]{2,1,0:T(2,128)(2,1)S(1)}, u32[]{:S(2)}, u32[]{:S(2)}) async-start(bf16[64,2,1280]{2,1,0:T(2,128)(2,1)} %reshape.83), calls=%async_computation.4 | async-start | bytes 655360 | tf_op jit(solution)/shard_map/all_to_all | solution.py:227
  179.7 9.6 %collective-permute-start.1 = (bf16[192,512]{1,0:T(8,128)(2,1)S(1)}, bf16[192,512]{1,0:T(8,128)(2,1)S(1)}, u32[]{:S(2)}, u32[]{:S(2)}) collective-permute-start(bf16[192,512]{1,0:T(8,128)(2,1)S(1)} %fusion.8), channel_id=1, source_target_pairs={{0,2},{2,4},{4,6},{6,0},{1,3},{3,5},{5,7},{7,1},{8,10},{10,12},{12... | collective-permute-start | bytes 589832 | tf_op jit(solution)/shard_map/ppermute | solution.py:223
  181.6 9.4 %collective-permute-start.2 = (bf16[192,512]{1,0:T(8,128)(2,1)S(1)}, bf16[192,512]{1,0:T(8,128)(2,1)S(1)}, u32[]{:S(2)}, u32[]{:S(2)}) collective-permute-start(bf16[192,512]{1,0:T(8,128)(2,1)S(1)} %fusion.8), channel_id=1, source_target_pairs={{0,4},{2,6},{4,0},{6,2},{1,5},{3,7},{5,1},{7,3},{8,12},{10,14},{12... | collective-permute-start | bytes 589832 | tf_op jit(solution)/shard_map/ppermute | solution.py:223
  186.0 9.0 %collective-permute-start.3 = (bf16[192,512]{1,0:T(8,128)(2,1)S(1)}, bf16[192,512]{1,0:T(8,128)(2,1)S(1)}, u32[]{:S(2)}, u32[]{:S(2)}) collective-permute-start(bf16[192,512]{1,0:T(8,128)(2,1)S(1)} %fusion.8), channel_id=1, source_target_pairs={{0,6},{2,0},{4,2},{6,4},{1,7},{3,1},{5,3},{7,5},{8,14},{10,8},{12,... | collective-permute-start | bytes 589832 | tf_op jit(solution)/shard_map/ppermute | solution.py:223
  195.1 3.6 %collective-permute-start.4 = (f32[192,512]{1,0:T(8,128)S(1)}, f32[192,512]{1,0:T(8,128)S(1)}, u32[]{:S(2)}, u32[]{:S(2)}) collective-permute-start(f32[192,512]{1,0:T(8,128)S(1)} %convert_add_fusion.3), channel_id=1, source_target_pairs={{0,1},{1,0},{2,3},{3,2},{4,5},{5,4},{6,7},{7,6},{8,9},{9,8},{10,11... | collective-permute-start | bytes 1179656 | tf_op jit(solution)/shard_map/ppermute | solution.py:270

commit v2 on v1

--- a/solution.py
+++ b/solution.py
@@ -8,6 +8,8 @@
 HEADS = 8
 EPS = 1e-05
 CAP = 8
+Y, Z, X = 4, 16, 4
+PIECE = 20
 BF = jnp.bfloat16
 F32 = jnp.float32
 TABLE = ("y", "z")
@@ -76,23 +78,92 @@
     )(asked, table)
 
 
-def collect_kernel(asked_ref, grads_ref, sum_ref):
-    chosen = chosen_rows(asked_ref, sum_ref.shape[0])
-    sum_ref[...] = dot(chosen, grads_ref[...], ((0,), (0,))).astype(sum_ref.dtype)
+def collect_kernel(asked_ref, grads_ref, mine_ref, other_ref, total):
+    half = mine_ref.shape[0]
+    chosen = chosen_rows(asked_ref, 2 * half)
+    total[...] = dot(chosen, grads_ref[...], ((0,), (0,)))
+    core = lax.axis_index("c")
+    for half_ref, c in ((mine_ref, core), (other_ref, 1 - core)):
+        half_ref[...] = total[pl.ds(pl.multiple_of(c * half, half), half), :].astype(BF)
 
 
 def collect(asked, grads, vocab_rows):
+    half = jax.ShapeDtypeStruct((vocab_rows // 2, grads.shape[1]), BF)
     return pl.pallas_call(
         collect_kernel,
-        out_shape=jax.ShapeDtypeStruct((vocab_rows, grads.shape[1]), BF),
+        out_shape=(half, half),
+        scratch_shapes=[pltpu.VMEM((vocab_rows, grads.shape[1]), F32)],
         name="collect",
     )(asked, grads)
 
 
+def place_kernel(mine_ref, other_ref, whole_ref):
+    half = mine_ref.shape[0]
+    core = lax.axis_index("c")
+    whole_ref[pl.ds(pl.multiple_of(core * half, half), half), :] = mine_ref[...]
+    whole_ref[pl.ds(pl.multiple_of((1 - core) * half, half), half), :] = other_ref[...]
+
+
+def place(mine, other):
+    return pl.pallas_call(
+        place_kernel,
+        out_shape=jax.ShapeDtypeStruct((2 * mine.shape[0], mine.shape[1]), F32),
+        name="place",
+    )(mine, other)
+
+
+def split_kernel(arrived_ref, pieces_ref):
+    _, size, _ = arrived_ref.shape
+    total = jnp.sum(arrived_ref[...].astype(F32), axis=0)
+    for z in range(size // PIECE):
+        pieces_ref[z] = total[z * PIECE : (z + 1) * PIECE].astype(BF)
+
+
+def split(arrived):
+    _, size, lanes = arrived.shape
+    return pl.pallas_call(
+        split_kernel,
+        out_shape=jax.ShapeDtypeStruct((size // PIECE, PIECE, lanes), BF),
+        name="split",
+    )(arrived)
+
+
+def spread_kernel(arrived_ref, copies_ref):
+    total = jnp.sum(arrived_ref[...].astype(F32), axis=0).astype(BF)
+    copies_ref[...] = jnp.broadcast_to(total[None], copies_ref.shape)
+
+
+def spread(arrived, copies):
+    return pl.pallas_call(
+        spread_kernel,
+        out_shape=jax.ShapeDtypeStruct((copies,) + arrived.shape[1:], BF),
+        name="spread",
+    )(arrived)
+
+
+def finish_kernel(pieces_ref, in_ref, out_ref):
+    flat = jnp.concatenate([pieces_ref[k].astype(F32) for k in range(pieces_ref.shape[0])], axis=0)
+    in_ref[:, :128] = flat[:512]
+    in_ref[:, 128:] = flat[512:1024]
+    for j in range(4):
+        out_ref[:, 128 * j : 128 * (j + 1)] = flat[1024 + 64 * j : 1088 + 64 * j]
+
+
+def finish(pieces):
+    return pl.pallas_call(
+        finish_kernel,
+        out_shape=(
+            jax.ShapeDtypeStruct((512, 256), F32),
+            jax.ShapeDtypeStruct((64, 512), F32),
+        ),
+        name="finish",
+    )(pieces)
+
+
 def layer_kernel(
     slot_ref, segment_ref, returned_ref, w_in_ref, w_out_ref, cot_ref,
-    out_ref, d_in_ref, d_out_ref, sent_ref,
-    mixed, slope, attended, d_mixed,
+    out_ref, sent_ref, mine_ref, other_ref,
+    mixed, slope, attended, d_mixed, d_out,
 ):
     rows, width = cot_ref.shape
     slots = returned_ref.shape[0]
@@ -148,7 +219,7 @@
     gated = (hat_a * gate).astype(BF)
     out_ref[...] = (embedded + dot(gated, w_out_ref[...])).astype(BF)
     cot = cot_ref[...]
-    d_out_ref[...] = dot(gated, cot, ((0,), (0,))).astype(BF)
+    d_out[...] = dot(gated, cot, ((0,), (0,)))
     d_gated = dot(cot, w_out_ref[...], ((1,), (1,))).astype(BF).astype(F32)
     d_mixed[:, :width] = ((d_gated * hat_a).astype(BF).astype(F32) * slope[:, :width]).astype(BF)
     d_hat = d_gated * gate
@@ -182,7 +253,6 @@
             whole = jnp.where(low, found[0][part], found[1][part]).astype(BF).astype(F32)
             d_mixed[:, span] = (whole * slope[:, span]).astype(BF)
     d_all = d_mixed[...]
-    d_in_ref[...] = dot(normed, d_all, ((0,), (0,))).astype(BF)
     d_normed = dot(d_all, w_in_ref[...], ((1,), (1,))).astype(BF).astype(F32)
     d_emb = inverse * (
         d_normed
@@ -191,6 +261,18 @@
     )
     d_emb = (cot.astype(F32) + d_emb).astype(BF)
     sent_ref[...] = dot(match, d_emb).astype(BF)
+    core = lax.axis_index("c")
+    for block_ref, c in ((mine_ref, core), (other_ref, 1 - core)):
+        for k in range(X):
+            d = 2 * k + c
+            columns = pl.ds(pl.multiple_of(d * 256, 256), 256)
+            d_in = dot(normed, d_mixed[:, columns], ((0,), (0,))).astype(BF)
+            d_rows = d_out[pl.ds(pl.multiple_of(d * 64, 64), 64), :].astype(BF)
+            parts_of = [d_in[:, :128], d_in[:, 128:]]
+            parts_of += [d_rows[:, 128 * j : 128 * (j + 1)] for j in range(4)]
+            block = jnp.concatenate(parts_of, axis=0)
+            for y in range(Y):
+                block_ref[y, k] = block[y * 320 : (y + 1) * 320]
 
 
 def layer(slot, segment, returned, w_in, w_out, cot):
@@ -199,82 +281,56 @@
         layer_kernel,
         out_shape=(
             jax.ShapeDtypeStruct((rows, width), BF),
-            jax.ShapeDtypeStruct(w_in.shape, BF),
-            jax.ShapeDtypeStruct(w_out.shape, BF),
             jax.ShapeDtypeStruct(returned.shape, BF),
+            jax.ShapeDtypeStruct((Y, X, 320, 128), BF),
+            jax.ShapeDtypeStruct((Y, X, 320, 128), BF),
         ),
         scratch_shapes=[
             pltpu.VMEM((rows, 4 * width), BF),
             pltpu.VMEM((rows, 4 * width), F32),
             pltpu.VMEM((rows, width), F32),
             pltpu.VMEM((rows, 4 * width), BF),
+            pltpu.VMEM((width, width), F32),
         ],
         name="layer",
     )(slot, segment, returned, w_in, w_out, cot)
 
 
-def share_sum_kernel(own_ref, a_ref, b_ref, c_ref, sum_ref):
-    total = own_ref[...].astype(F32) + a_ref[...].astype(F32)
-    total = total + b_ref[...].astype(F32) + c_ref[...].astype(F32)
-    sum_ref[...] = total.astype(sum_ref.dtype)
-
-
-def shift(x, axis, by, size):
-    return lax.ppermute(x, axis, [(i, (i + by) % size) for i in range(size)])
-
-
 def exchange(x, axes):
     return lax.all_to_all(x, axes, split_axis=0, concat_axis=0, tiled=True)
 
 
-def part_of(x, index):
-    return lax.dynamic_index_in_dim(x, index, 0, keepdims=False)
-
-
 def on_device(table, owner, row_in_shard, segment, w_in, w_out, cotangent):
-    shards = 64
+    shards = Y * Z
     vocab_rows, width = table.shape
     rows = owner.shape[1]
-    x, c = lax.axis_index("x"), lax.axis_index("c")
     request, slot = plan(owner.reshape(1, rows), row_in_shard, shards)
     asked = exchange(request.reshape(shards, 1, 128), TABLE).reshape(shards, 128)
     found = serve(asked, table)
     returned = exchange(found.reshape(shards, CAP, width), TABLE).reshape(shards * CAP, width)
-    out, d_in, d_out, sent = layer(slot, segment, returned, w_in, w_out, cotangent[0])
-    blocks = jnp.concatenate(
-        [
-            d_in.reshape(width, 4, 2, 256).transpose(1, 2, 0, 3).reshape(4, 2, 256, 512),
-            d_out.reshape(4, 2, 64, 512),
-        ],
-        axis=2,
-    )
-    mine = lax.dynamic_index_in_dim(blocks, c, 1, keepdims=False)
-    other = lax.dynamic_index_in_dim(blocks, 1 - c, 1, keepdims=False)
+    out, sent, mine, other = layer(slot, segment, returned, w_in, w_out, cotangent[0])
     other = lax.ppermute(other, "c", [(0, 1), (1, 0)])
+    arrived = exchange(sent.reshape(shards, CAP, width), TABLE)
+    arrived = arrived.reshape(shards * CAP, width)
     halves = (mine.astype(F32) + other.astype(F32)).astype(BF)
-    arrived = exchange(sent.reshape(shards, CAP, width), TABLE).reshape(shards * CAP, width)
-    pieces = [part_of(halves, x)] + [
-        shift(part_of(halves, (x + k) % 4), "x", k, 4) for k in (1, 2, 3)
-    ]
-    share = sum(p.astype(F32) for p in pieces)
-    share = exchange(share.astype(BF).reshape(shards, 2560), TABLE)
-    share = jnp.sum(share.astype(F32), axis=0).astype(BF)
-    share = exchange(jnp.broadcast_to(share[None], (shards, 2560)), TABLE).astype(F32)
-    share = share.reshape(320, 512)
-    part = collect(asked, arrived, vocab_rows)
-    part = part.reshape(2, 192, width)
-    other = lax.ppermute(part_of(part, 1 - c), "c", [(0, 1), (1, 0)])
-    half = (part_of(part, c).astype(F32) + other.astype(F32)).astype(BF)
-    halves = [half] + [shift(half, "x", k, 4) for k in (1, 2, 3)]
-    half = sum(h.astype(F32) for h in halves)
-    other = lax.ppermute(half, "c", [(0, 1), (1, 0)])
-    grad_table = jnp.where(c == 0, jnp.concatenate([half, other]), jnp.concatenate([other, half]))
-    return out[None], grad_table, share[:256].reshape(512, 256), share[256:]
+    share = exchange(halves.reshape(Y * X, 320, 128), ("y", "x"))
+    share = exchange(split(share), "z")
+    share = exchange(spread(share, shards), TABLE)
+    grad_in, grad_out = finish(share)
+    mine, other = collect(asked, arrived, vocab_rows)
+    other = lax.ppermute(other, "c", [(0, 1), (1, 0)])
+    mine = (mine.astype(F32) + other.astype(F32)).astype(BF)
+    other = lax.ppermute(mine, "x", [(0, 3), (1, 2), (2, 1), (3, 0)])
+    mine = (mine.astype(F32) + other.astype(F32)).astype(BF)
+    other = lax.ppermute(mine, "x", [(0, 1), (1, 0), (2, 3), (3, 2)])
+    mine = mine.astype(F32) + other.astype(F32)
+    other = lax.ppermute(mine, "c", [(0, 1), (1, 0)])
+    grad_table = place(mine, other)
+    return out[None], grad_table, grad_in, grad_out
 
 
 def solution(mesh):
-    devices = mesh.devices
-    grid = Mesh(devices.reshape(4, 16, 4, 2), ALL)
+    grid = Mesh(mesh.devices.reshape(Y, Z, X, 2), ALL)
     placed = (
         P(TABLE, None),
         P(ALL, None, None),

time: 208 us -> 209 us (level)
  blocking collectives: 33.1 us -> 93.6 us
  starting transfers between devices: 53.1 us -> 28.3 us
  waiting for transfers between devices: 77 us -> 55.7 us
  local copies, waits for them, and re-layouts: 14.5 us -> 2.15 us
  other arithmetic: 11.7 us -> 1.81 us
  Pallas kernels: 16.1 us -> 24.7 us
    all_to_all x1 -> x3, blocking collectives: 33.1 us -> 93.6 us  [exchange(): return lax.all_to_all(x, axes, split_axis=0, concat_axis=0, tiled=True)]
    all_to_all x4 -> x3, waiting for transfers between devices: 56.1 us -> 39.3 us  [exchange(): return lax.all_to_all(x, axes, split_axis=0, concat_axis=0, tiled=True)]
    ppermute x8 -> x3, starting transfers between devices: 22.4 us -> 8.09 us  [the longest x1 3.97 us: on_device(): other = lax.ppermute(mine, 'x', [(0, 3), (1, 2), (2, 1), (3, 0)])]
    all_to_all x4 -> x3, starting transfers between devices: 28.9 us -> 16.3 us  [exchange(): return lax.all_to_all(x, axes, split_axis=0, concat_axis=0, tiled=True)]
    reshape x4 -> x0, local copies, waits for them, and re-layouts: 8.63 us -> none  [the longest x3 7.76 us: on_device(): d_in.reshape(width, 4, 2, 256).transpose(1, 2, 0, 3).reshape(4, 2, 256, 512)]
    pallas_call x1 -> x5, Pallas kernels: 2.34 us -> 10.2 us  [the longest x1 2.42 us: collect(): pl.pallas_call(collect_kernel, out_shape=(half, half), scratch_shapes=[pl...]
    ppermute x8 -> x3, waiting for transfers between devices: 20.9 us -> 13.2 us  [the longest x1 5.91 us: on_device(): other = lax.ppermute(mine, 'x', [(0, 3), (1, 2), (2, 1), (3, 0)])]
    ppermute x1 -> x2, waiting for transfers between devices: 0.01 us -> 3.21 us  [on_device(): other = lax.ppermute(other, 'c', [(0, 1), (1, 0)])]
  transfers between devices with their start and end apart: 13 -> 8, of which waited for: 10 -> 7; matrix products, arithmetic and copies ran while one was open for 6% -> 0% of each run, Pallas kernels for 1% -> 4%
where the time goes in v2:
time: 209 us; the launch traced here: 207 us
  blocking collectives  93.6 us (45%)
  waiting for transfers between devices  55.7 us (27%)
  starting transfers between devices  28.3 us (14%)
  Pallas kernels  24.7 us (12%)
  local copies, waits for them, and re-layouts  2.15 us (1%)
    all_to_all x3, blocking collectives, exchange(): return lax.all_to_all(x, axes, split_axis=0, concat_axis=0, tiled=True)  93.6 us
    all_to_all x3, waiting for transfers between devices, exchange(): return lax.all_to_all(x, axes, split_axis=0, concat_axis=0, tiled=True)  39.3 us
    all_to_all x3, starting transfers between devices, exchange(): return lax.all_to_all(x, axes, split_axis=0, concat_axis=0, tiled=True)  16.3 us
    pallas_call x1, Pallas kernels, layer(): pl.pallas_call(layer_kernel, out_shape=(jax.ShapeDtypeStruct((rows, width...  10.6 us
    ppermute x1, waiting for transfers between devices, on_device(): other = lax.ppermute(mine, 'x', [(0, 3), (1, 2), (2, 1), (3, 0)])  5.91 us
    ppermute x1, waiting for transfers between devices, on_device(): other = lax.ppermute(mine, 'x', [(0, 1), (1, 0), (2, 3), (3, 2)])  5.61 us
  transfers between devices with their start and end apart: 8, of which 7 were waited for; matrix products, arithmetic and copies ran while one was open for 0% of the time, Pallas kernels for 4%

profile of v2, /device:TPU:6, one launch (start us, length us, event | category | flops | bytes accessed | tf_op | source)
XLA Modules:
  0.0 207.0 jit_solution(17483614110294794652)
XLA Ops:
  2.2 33.2 %all_to_all.30 = s32[64,1,128]{2,1,0:T(1,128)} all-to-all(s32[64,1,128]{2,1,0:T(1,128)} %bitcast.19), channel_id=1, replica_groups=mesh['y'=4,'z'=16,'x'=4,'c'=2] {'y','z'}, dimensions={0} | all-to-all | bytes 65536 | tf_op jit(solution)/shard_map/all_to_all | solution.py:300
  35.4 2.3 %serve.1 = bf16[512,512]{1,0:T(8,128)(2,1)} custom-call(s32[64,128]{1,0:T(8,128)} %bitcast.16, bf16[384,512]{1,0:T(8,128)(2,1)} %table_ref.1), custom_call_target="tpu_custom_call" | custom-call | tf_op jit(solution)/shard_map/serve/pallas_call | solution.py:74
  37.7 35.9 %all_to_all.31 = bf16[64,8,512]{2,1,0:T(8,128)(2,1)} all-to-all(bf16[64,8,512]{2,1,0:T(8,128)(2,1)} %bitcast.14), channel_id=1, replica_groups=mesh['y'=4,'z'=16,'x'=4,'c'=2] {'y','z'}, dimensions={0} | all-to-all | bytes 1048576 | tf_op jit(solution)/shard_map/all_to_all | solution.py:300
  73.6 10.6 %layer.1 = (bf16[256,512]{1,0:T(8,128)(2,1)}, bf16[512,512]{1,0:T(8,128)(2,1)}, bf16[4,4,320,128]{3,2,1,0:T(8,128)(2,1)}, bf16[4,4,320,128]{3,2,1,0:T(8,128)(2,1)}) custom-call(s32[1,256]{1,0:T(1,128)} %get-tuple-element.14.slot_ref, s32[1,256]{1,0:T(1,128)} %segment_ref.1, bf16[512,512]{1,0:T(8,128)(2,1)} %bitcast.15, bf16[512,2048]{1,0:T(8,128)(2,1)} %w_in_ref.1, ...), custom_call_target="tpu_custom_call" | custom-call | tf_op jit(solution)/shard_map/layer/pallas_call | solution.py:280
  84.2 1.9 collective-permute-start.4
  86.1 3.2 %collective-permute-done.4 = bf16[4,4,320,128]{3,2,1,0:T(8,128)(2,1)S(1)} collective-permute-done((bf16[4,4,320,128]{3,2,1,0:T(8,128)(2,1)}, bf16[4,4,320,128]{3,2,1,0:T(8,128)(2,1)S(1)}, u32[]{:S(2)}, u32[]{:S(2)}) %collective-permute-start.4) | collective-permute-done | bytes 1310752 | tf_op jit(solution)/shard_map/ppermute | solution.py:312
  91.0 24.5 %all_to_all.32.arrived_ref = bf16[16,320,128]{2,1,0:T(8,128)(2,1)} all-to-all(bf16[16,320,128]{2,1,0:T(8,128)(2,1)S(1)} %bitcast.12), channel_id=1, replica_groups=mesh['y'=4,'z'=16,'x'=4,'c'=2] {'y','x'}, dimensions={0} | all-to-all | bytes 2621440 | tf_op jit(solution)/shard_map/all_to_all | solution.py:300
  115.5 5.6 %all-to-all-start.2 = ((bf16[64,8,512]{2,1,0:T(8,128)(2,1)}), bf16[64,8,512]{2,1,0:T(8,128)(2,1)S(1)}, u32[]{:S(2)}, u32[]{:S(2)}) async-start(bf16[64,8,512]{2,1,0:T(8,128)(2,1)} %bitcast.8), calls=%async_computation.2 | async-start | bytes 1048576 | tf_op jit(solution)/shard_map/all_to_all | solution.py:300
  121.1 2.1 %split.1 = bf16[16,20,128]{2,1,0:T(8,128)(2,1)} custom-call(bf16[16,320,128]{2,1,0:T(8,128)(2,1)} %all_to_all.32.arrived_ref), custom_call_target="tpu_custom_call" | custom-call | tf_op jit(solution)/shard_map/split/pallas_call | solution.py:124
  123.2 28.3 %all-to-all-done.2 = bf16[64,8,512]{2,1,0:T(8,128)(2,1)S(1)} async-done(((bf16[64,8,512]{2,1,0:T(8,128)(2,1)}), bf16[64,8,512]{2,1,0:T(8,128)(2,1)S(1)}, u32[]{:S(2)}, u32[]{:S(2)}) %all-to-all-start.2) | async-done | bytes 524320 | tf_op jit(solution)/shard_map/all_to_all | solution.py:300
  151.5 5.7 %all-to-all-start.4 = ((bf16[16,20,128]{2,1,0:T(8,128)(2,1)}), bf16[16,20,128]{2,1,0:T(8,128)(2,1)S(1)}, u32[]{:S(2)}, u32[]{:S(2)}) async-start(bf16[16,20,128]{2,1,0:T(8,128)(2,1)} %split.1), calls=%async_computation.4 | async-start | bytes 196608 | tf_op jit(solution)/shard_map/all_to_all | solution.py:300
  157.3 2.4 %collect.1 = (bf16[192,512]{1,0:T(8,128)(2,1)}, bf16[192,512]{1,0:T(8,128)(2,1)}) custom-call(s32[64,128]{1,0:T(8,128)} %bitcast.17, bf16[512,512]{1,0:T(8,128)(2,1)} %bitcast.13), custom_call_target="tpu_custom_call" | custom-call | tf_op jit(solution)/shard_map/collect/pallas_call | solution.py:92
  159.7 2.0 collective-permute-start
  161.8 8.6 %all-to-all-done.4.arrived_ref = bf16[16,20,128]{2,1,0:T(8,128)(2,1)S(1)} async-done(((bf16[16,20,128]{2,1,0:T(8,128)(2,1)}), bf16[16,20,128]{2,1,0:T(8,128)(2,1)S(1)}, u32[]{:S(2)}, u32[]{:S(2)}) %all-to-all-start.4) | async-done | bytes 81952 | tf_op jit(solution)/shard_map/all_to_all | solution.py:300
  171.0 1.7 spread.1
  172.7 4.9 %all-to-all-start.5 = ((bf16[64,20,128]{2,1,0:T(8,128)(2,1)}), bf16[64,20,128]{2,1,0:T(8,128)(2,1)S(1)}, u32[]{:S(2)}, u32[]{:S(2)}) async-start(bf16[64,20,128]{2,1,0:T(8,128)(2,1)} %spread.1), calls=%async_computation.5 | async-start | bytes 786432 | tf_op jit(solution)/shard_map/all_to_all | solution.py:300
  177.7 4.0 %collective-permute-start.1 = (bf16[192,512]{1,0:T(8,128)(2,1)S(1)}, bf16[192,512]{1,0:T(8,128)(2,1)S(1)}, u32[]{:S(2)}, u32[]{:S(2)}) collective-permute-start(bf16[192,512]{1,0:T(8,128)(2,1)S(1)} %add_convert_fusion.2), channel_id=1, source_target_pairs={{0,6},{2,4},{4,2},{6,0},{1,7},{3,5},{5,3},{7,1},{8,14},{10,12},{12... | collective-permute-start | bytes 589832 | tf_op jit(solution)/shard_map/ppermute | solution.py:323
  181.7 5.9 %collective-permute-done.1 = bf16[192,512]{1,0:T(8,128)(2,1)S(1)} collective-permute-done((bf16[192,512]{1,0:T(8,128)(2,1)S(1)}, bf16[192,512]{1,0:T(8,128)(2,1)S(1)}, u32[]{:S(2)}, u32[]{:S(2)}) %collective-permute-start.1) | collective-permute-done | bytes 196640 | tf_op jit(solution)/shard_map/ppermute | solution.py:323
  187.6 2.2 %collective-permute-start.2 = (bf16[192,512]{1,0:T(8,128)(2,1)S(1)}, bf16[192,512]{1,0:T(8,128)(2,1)S(1)}, u32[]{:S(2)}, u32[]{:S(2)}) collective-permute-start(bf16[192,512]{1,0:T(8,128)(2,1)S(1)} %add_convert_fusion.1), channel_id=1, source_target_pairs={{0,2},{2,0},{4,6},{6,4},{1,3},{3,1},{5,7},{7,5},{8,10},{10,8},{12,... | collective-permute-start | bytes 589832 | tf_op jit(solution)/shard_map/ppermute | solution.py:325
  189.9 5.6 %collective-permute-done.2 = bf16[192,512]{1,0:T(8,128)(2,1)S(1)} collective-permute-done((bf16[192,512]{1,0:T(8,128)(2,1)S(1)}, bf16[192,512]{1,0:T(8,128)(2,1)S(1)}, u32[]{:S(2)}, u32[]{:S(2)}) %collective-permute-start.2) | collective-permute-done | bytes 196640 | tf_op jit(solution)/shard_map/ppermute | solution.py:325
  195.5 1.9 collective-permute-start.3
  199.9 2.1 place.1
  201.9 2.4 %all-to-all-done.5.pieces_ref = bf16[64,20,128]{2,1,0:T(8,128)(2,1)S(1)} async-done(((bf16[64,20,128]{2,1,0:T(8,128)(2,1)}), bf16[64,20,128]{2,1,0:T(8,128)(2,1)S(1)}, u32[]{:S(2)}, u32[]{:S(2)}) %all-to-all-start.5) | async-done | bytes 327712 | tf_op jit(solution)/shard_map/all_to_all | solution.py:300
  205.1 1.9 finish.1
  (19 shorter events, 7.2 us)
Async XLA Ops:
  84.2 5.1 %collective-permute-start.4 = (bf16[4,4,320,128]{3,2,1,0:T(8,128)(2,1)}, bf16[4,4,320,128]{3,2,1,0:T(8,128)(2,1)S(1)}, u32[]{:S(2)}, u32[]{:S(2)}) collective-permute-start(bf16[4,4,320,128]{3,2,1,0:T(8,128)(2,1)} %get-tuple-element.21), channel_id=1, source_target_pairs={{0,1},{1,0},{2,3},{3,2},{4,5},{5,4},{6,7},{7,6},{8,9},{9,8},{10,11... | collective-permute-start | bytes 3932168 | tf_op jit(solution)/shard_map/ppermute | solution.py:312
  115.5 36.1 %all-to-all-start.2 = ((bf16[64,8,512]{2,1,0:T(8,128)(2,1)}), bf16[64,8,512]{2,1,0:T(8,128)(2,1)S(1)}, u32[]{:S(2)}, u32[]{:S(2)}) async-start(bf16[64,8,512]{2,1,0:T(8,128)(2,1)} %bitcast.8), calls=%async_computation.2 | async-start | bytes 1048576 | tf_op jit(solution)/shard_map/all_to_all | solution.py:300
  151.5 5.8 %copy-start = (bf16[64,8,512]{2,1,0:T(8,128)(2,1)}, bf16[64,8,512]{2,1,0:T(8,128)(2,1)S(1)}, u32[]{:S(2)}) copy-start(bf16[64,8,512]{2,1,0:T(8,128)(2,1)S(1)} %all-to-all-done.2) | copy-start | bytes 1572868
  151.5 18.8 %all-to-all-start.4 = ((bf16[16,20,128]{2,1,0:T(8,128)(2,1)}), bf16[16,20,128]{2,1,0:T(8,128)(2,1)S(1)}, u32[]{:S(2)}, u32[]{:S(2)}) async-start(bf16[16,20,128]{2,1,0:T(8,128)(2,1)} %split.1), calls=%async_computation.4 | async-start | bytes 196608 | tf_op jit(solution)/shard_map/all_to_all | solution.py:300
  159.7 17.9 %copy-start.5 = (bf16[192,512]{1,0:T(8,128)(2,1)S(1)}, bf16[192,512]{1,0:T(8,128)(2,1)}, u32[]{:S(2)}) copy-start(bf16[192,512]{1,0:T(8,128)(2,1)} %get-tuple-element.18) | copy-start | bytes 589828
  159.7 17.9 %collective-permute-start = (bf16[192,512]{1,0:T(8,128)(2,1)}, bf16[192,512]{1,0:T(8,128)(2,1)S(1)}, u32[]{:S(2)}, u32[]{:S(2)}) collective-permute-start(bf16[192,512]{1,0:T(8,128)(2,1)} %get-tuple-element.19), channel_id=1, source_target_pairs={{0,1},{1,0},{2,3},{3,2},{4,5},{5,4},{6,7},{7,6},{8,9},{9,8},{10,11... | collective-permute-start | bytes 589832 | tf_op jit(solution)/shard_map/ppermute | solution.py:321
  170.3 0.6 copy-start.4
  172.7 31.7 %all-to-all-start.5 = ((bf16[64,20,128]{2,1,0:T(8,128)(2,1)}), bf16[64,20,128]{2,1,0:T(8,128)(2,1)S(1)}, u32[]{:S(2)}, u32[]{:S(2)}) async-start(bf16[64,20,128]{2,1,0:T(8,128)(2,1)} %spread.1), calls=%async_computation.5 | async-start | bytes 786432 | tf_op jit(solution)/shard_map/all_to_all | solution.py:300
  177.7 9.9 %collective-permute-start.1 = (bf16[192,512]{1,0:T(8,128)(2,1)S(1)}, bf16[192,512]{1,0:T(8,128)(2,1)S(1)}, u32[]{:S(2)}, u32[]{:S(2)}) collective-permute-start(bf16[192,512]{1,0:T(8,128)(2,1)S(1)} %add_convert_fusion.2), channel_id=1, source_target_pairs={{0,6},{2,4},{4,2},{6,0},{1,7},{3,5},{5,3},{7,1},{8,14},{10,12},{12... | collective-permute-start | bytes 589832 | tf_op jit(solution)/shard_map/ppermute | solution.py:323
  187.6 7.8 %collective-permute-start.2 = (bf16[192,512]{1,0:T(8,128)(2,1)S(1)}, bf16[192,512]{1,0:T(8,128)(2,1)S(1)}, u32[]{:S(2)}, u32[]{:S(2)}) collective-permute-start(bf16[192,512]{1,0:T(8,128)(2,1)S(1)} %add_convert_fusion.1), channel_id=1, source_target_pairs={{0,2},{2,0},{4,6},{6,4},{1,3},{3,1},{5,7},{7,5},{8,10},{10,8},{12,... | collective-permute-start | bytes 589832 | tf_op jit(solution)/shard_map/ppermute | solution.py:325
  195.5 3.6 %copy-start.2 = (f32[192,512]{1,0:T(8,128)}, f32[192,512]{1,0:T(8,128)S(1)}, u32[]{:S(2)}) copy-start(f32[192,512]{1,0:T(8,128)S(1)} %convert_add_fusion.mine_ref) | copy-start | bytes 1179652
  195.5 3.6 %collective-permute-start.3 = (f32[192,512]{1,0:T(8,128)S(1)}, f32[192,512]{1,0:T(8,128)S(1)}, u32[]{:S(2)}, u32[]{:S(2)}) collective-permute-start(f32[192,512]{1,0:T(8,128)S(1)} %convert_add_fusion.mine_ref), channel_id=1, source_target_pairs={{0,1},{1,0},{2,3},{3,2},{4,5},{5,4},{6,7},{7,6},{8,9},{9,8},{10,11... | collective-permute-start | bytes 1179656 | tf_op jit(solution)/shard_map/ppermute | solution.py:327
  199.1 0.7 copy-start.3
  204.3 0.8 copy-start.1
